TPU v7x, 256 devices: a whole 4x4x8 slice. The times are simulated.
256 devices in a mesh: expert: 32 (over x, y, core), group: 8 (over z).
Axes of the slice: x: 4, y: 4, z: 8, core: 2. Of those that a mesh axis runs over, the one named last changes fastest.
Arguments:
- tokens: bfloat16 [2048, 7168], P(('expert', 'group')), may hold values from -6 to 6
- routes: int32 [2048, 8], P(('expert', 'group')), may hold values from 0 to 31, all different within a row; in each aligned block of 8 rows (0 to 7, 8 to 15, ...) at most 4 rows name the same one
- gate_weight: bfloat16 [32, 7168, 2048], P('expert', None, 'group'), may hold values from -0.0625 to 0.0625
- up_weight: bfloat16 [32, 7168, 2048], P('expert', None, 'group'), may hold values from -0.0625 to 0.0625
- down_weight: bfloat16 [32, 2048, 7168], P('expert', 'group'), may hold values from -6 to 6
- merge_group: int32 [32], replicated, may hold values from 0 to 7, as said below
- neuron_perm: int32 [32, 2048], P('expert', 'group'), may hold values from 0 to 2047, as said below
Outputs:
- merged_down: bfloat16 [8, 2048, 7168], P(None, 'group', 'expert')
Inputs may be any that keep to these rules, and one draw needn't show every extreme that they name: `routes`: among the rows of one device (8 rows), no expert is named by more than 4 rows. `merge_group`: every one of the 8 merge groups has at least one expert. `neuron_perm`: each row is a permutation of 0 to 2047 that keeps every hidden unit within its aligned block of 128.
All inputs are finite; a program needn't handle non-finite values.
Results may differ from a plain program's by a relative error of at most 0.0047.
Values may be sent and summed in bfloat16 or wider, within the bound.
A program may use at most 128 MiB of HBM per device.

v0:
```python
from functools import partial
import jax
import jax.numpy as jnp
from jax import lax
from jax.sharding import PartitionSpec as P

TOP = 8
NB = 128
off_weight = 0.75
ridge_eps = 1e-05


def make_slots(block_routes, block_tokens, experts, capacity):
    row_count = block_tokens.shape[0]
    flat_routes = block_routes.reshape(-1)
    onehot = (flat_routes[:, None] == jnp.arange(experts, dtype=jnp.int32)[None, :]).astype(
        jnp.int32
    )
    position = jnp.sum((jnp.cumsum(onehot, axis=0) - 1) * onehot, axis=1)
    target = flat_routes * capacity + position
    matches = target[None, :] == jnp.arange(experts * capacity, dtype=jnp.int32)[:, None]
    chooser = jnp.sum(
        matches.reshape(experts * capacity, row_count, -1).astype(jnp.float32), axis=2
    ).astype(jnp.bfloat16)
    return jnp.dot(chooser, block_tokens, preferred_element_type=jnp.float32).astype(jnp.bfloat16)


def activate(shard_piece, gate_weight, up_weight):
    gate_part = jnp.einsum(
        "ksjcd,jdf->ksjcf", shard_piece, gate_weight, preferred_element_type=jnp.float32
    )
    up_part = jnp.einsum(
        "ksjcd,jdf->ksjcf", shard_piece, up_weight, preferred_element_type=jnp.float32
    )
    return (jax.nn.silu(gate_part) * up_part).astype(jnp.bfloat16)


def build_system(summed):
    unit_matrix = jnp.eye(summed.shape[-1], dtype=jnp.float32)
    return (
        off_weight * summed + (1.0 - off_weight) * (summed * unit_matrix) + ridge_eps * unit_matrix
    )


def make_inverse(factor):
    unit_matrix = jnp.broadcast_to(jnp.eye(factor.shape[-1], dtype=jnp.float32), factor.shape)
    lower_inverse = lax.linalg.triangular_solve(factor, unit_matrix, left_side=True, lower=True)
    return jnp.einsum(
        "mbki,mbkj->mbij", lower_inverse, lower_inverse, precision=lax.Precision.HIGHEST
    )


def apply_inverse(inverse, right_side):
    return jnp.einsum("mbik,mbkd->mbid", inverse, right_side, precision=lax.Precision.HIGHEST)


def per_device(tokens, routes, gate_weight, up_weight, down_weight, merge_group, neuron_perm):
    expert_count = lax.axis_size("expert")
    group_count = lax.axis_size("group")
    local_experts = gate_weight.shape[0]
    experts = expert_count * local_experts
    row_count = tokens.shape[0]
    width = tokens.shape[1]
    unit_count = gate_weight.shape[2]
    capacity = max(2, row_count * TOP * 2 // (experts * local_experts))
    block_count = unit_count // NB
    column_count = width // expert_count
    groups = experts // 4
    slot_maker = partial(make_slots, experts=experts, capacity=capacity)
    own_slots = slot_maker(routes, tokens).reshape(expert_count, local_experts * capacity, width)
    arrived = lax.all_to_all(own_slots, "expert", split_axis=0, concat_axis=0, tiled=True)
    hidden = activate(
        lax.all_gather(
            arrived.reshape(1, expert_count, local_experts, capacity, width),
            "group",
            axis=0,
            tiled=True,
        ),
        gate_weight,
        up_weight,
    )
    hidden = hidden.reshape(group_count, expert_count, local_experts, capacity, block_count, NB)
    within = (
        neuron_perm.reshape(local_experts, block_count, NB) - lax.axis_index("group") * unit_count
    )
    within = within - (jnp.arange(block_count, dtype=jnp.int32) * NB)[None, :, None]
    selector = (
        within[:, :, None, :] == jnp.arange(NB, dtype=jnp.int32)[None, None, :, None]
    ).astype(jnp.bfloat16)
    aligned = jnp.einsum(
        "gejcbi,jbin->gejcbn", hidden, selector, preferred_element_type=jnp.float32
    ).astype(jnp.bfloat16)
    gram = jnp.einsum("gejcbi,gejcbk->jbik", aligned, aligned, preferred_element_type=jnp.float32)
    moved_rows = jnp.einsum(
        "jbin,jbid->jbnd",
        selector,
        down_weight.reshape(local_experts, block_count, NB, width),
        preferred_element_type=jnp.float32,
    )
    term_part = jnp.einsum("jbni,jbid->jbnd", gram, moved_rows, precision=lax.Precision.HIGHEST)
    owner_index = lax.axis_index("expert")
    own_groups = lax.dynamic_slice_in_dim(merge_group, owner_index * local_experts, local_experts)
    own_onehot = (own_groups[:, None] == jnp.arange(groups, dtype=jnp.int32)[None, :]).astype(
        jnp.float32
    )
    placed = jnp.einsum("jm,jbik->mbik", own_onehot, gram, precision=lax.Precision.HIGHEST)
    group_gram = lax.psum(placed, "expert")
    inverse = make_inverse(jnp.linalg.cholesky(build_system(group_gram)))
    shaped_terms = term_part.reshape(local_experts, block_count, NB, expert_count, column_count)
    collected = lax.all_to_all(shaped_terms, "expert", split_axis=3, concat_axis=0, tiled=True)
    all_onehot = (merge_group[:, None] == jnp.arange(groups, dtype=jnp.int32)[None, :]).astype(
        jnp.float32
    )
    summed = jnp.einsum(
        "em,ebnd->mbnd", all_onehot, collected[:, :, :, 0, :], precision=lax.Precision.HIGHEST
    )
    merged = apply_inverse(inverse, summed)
    return merged.reshape(groups, unit_count, column_count).astype(jnp.bfloat16)


def solution(mesh):
    in_specs = (
        P(("expert", "group"), None),
        P(("expert", "group"), None),
        P("expert", None, "group"),
        P("expert", None, "group"),
        P("expert", "group", None),
        P(),
        P("expert", "group"),
    )
    out_specs = P(None, "group", "expert")
    return jax.shard_map(
        per_device, mesh=mesh, in_specs=in_specs, out_specs=out_specs, check_vma=False
    )
```

profile of v0, /device:TPU:1, one launch (start us, length us, event | category | flops | bytes accessed | tf_op | source)
XLA Modules:
  0.0 783.2 jit_solution(4557623676575485270)
XLA Ops:
  6.5 0.0 copy-start
  6.5 0.0 all-gather.3.cloned.1.call-start
  6.5 0.8 eq.91
  7.3 0.1 fusion.51
  7.4 0.1 reduce_window_sum.11
  7.5 0.2 select_reduce_fusion.1
  7.7 0.1 reduce_sum.21
  7.8 0.7 multiply_add_fusion
  8.5 0.1 convert_reduce_fusion
  8.6 0.0 copy-done
  8.6 0.7 convolution_convert_fusion
  9.3 1.7 reshape.138
  10.9 34.1 %all_to_all.20 = bf16[32,4,7168]{2,1,0:T(4,128)(2,1)S(1)} all-to-all(bf16[32,4,7168]{2,1,0:T(4,128)(2,1)} %reshape.138), channel_id=1, replica_groups=mesh['expert'=32,'group'=8] {'expert'}, dimensions={0} | all-to-all | bytes 3670016 | tf_op jit(solution)/shard_map/all_to_all | solution.py:71
  45.0 0.0 copy-start.3
  45.0 1.8 copy.66
  46.8 0.0 all-gather.3.cloned.1.call-update
  46.8 0.0 copy-done.3
  46.9 0.1 broadcast_subtract_fusion
  46.9 6.1 fusion.44
  53.1 145.8 %all-gather.3.cloned.1.call-done = bf16[256,4,7168]{2,0,1:T(8,128)(2,1)} async-done(((bf16[32,4,7168]{2,0,1:T(8,128)(2,1)}), bf16[256,4,7168]{2,0,1:T(8,128)(2,1)}) %all-gather.3.cloned.1.call-update) | async-done | bytes 14680080 | tf_op jit(solution)/shard_map/all_gather | solution.py:73
  198.9 0.0 copy-start.5
  198.9 8.5 %fusion.14 = f32[8,32,1,4,256]{4,1,3,0,2:T(8,128)S(1)} fusion(bf16[1,7168,256]{2,1,0:T(8,128)(2,1)} %param.9, bf16[8,32,4,7168]{3,1,0,2:T(8,128)(2,1)} %bitcast.99), kind=kOutput, calls=%fused_computation.13 | convolution fusion | flops 3758096384 | bytes 19398656 | tf_op jit(solution)/shard_map/ksjcd,jdf->ksjcf/dot_general | solution.py:29
  207.4 1.9 copy-done.5
  209.3 6.0 fusion.32
  215.3 0.1 reshape.143
  215.5 0.4 fusion.37
  215.8 0.3 convolution_bitcast_fusion
  216.2 14.0 %fusion.57 = f32[2,128,7168]{1,2,0:T(8,128)S(1)} fusion(f32[2,128,128]{2,1,0:T(8,128)S(1)} %convolution_bitcast_fusion, f32[2,128,7168]{2,1,0:T(8,128)} %fusion.44), kind=kOutput, calls=%fused_computation.58 | convolution fusion | flops 2818572288 | bytes 14811136 | tf_op jit(solution)/shard_map/jbni,jbid->jbnd/dot_general | solution.py:100
  230.2 3.7 copy.83
  233.9 0.0 copy-start.4
  233.9 7.9 %all-to-all-start.1 = ((f32[1,2,128,32,224]{2,4,1,0,3:T(8,128)}), f32[1,2,128,32,224]{2,4,1,0,3:T(8,128)}, u32[]{:S(2)}, u32[]{:S(2)}) async-start(f32[1,2,128,32,224]{2,4,1,0,3:T(8,128)} %copy.83), calls=%async_computation.1 | async-start | bytes 14680064 | tf_op jit(solution)/shard_map/all_to_all | solution.py:110
  241.8 0.0 all-reduce.2.cloned.1.call-start
  241.8 0.0 copy-done.4
  241.8 0.6 dynamic_slice.3
  242.4 0.6 compare_convert_fusion
  243.1 0.1 copy.73
  243.2 1.2 broadcast_multiply_fusion
  244.3 0.0 all-reduce.2.cloned.1.call-update
  244.4 0.1 copy.74
  244.5 0.1 copy.75
  244.6 167.6 %all-reduce.2.cloned.1.call-done = f32[8,2,128,128]{2,3,1,0:T(8,128)} async-done(((f32[8,2,128,128]{2,3,1,0:T(8,128)}), f32[8,2,128,128]{2,3,1,0:T(8,128)}) %all-reduce.2.cloned.1.call-update) | async-done | bytes 1048592 | tf_op jit(solution)/shard_map/psum | solution.py:107
  412.2 0.0 copy-start.2
  412.2 1.5 add_add_fusion
  413.7 0.3 copy.76
  414.1 0.0 copy-done.2
  414.1 0.2 fusion.40
  414.3 187.8 %custom-call.7 = f32[8,2,128,128]{3,2,1,0:T(8,128)S(1)} custom-call(f32[8,2,128,128]{3,2,1,0:T(8,128)S(1)} %fusion.40), custom_call_target="Cholesky" | custom-call | tf_op jit(solution)/shard_map/jit(cholesky)/cholesky | solution.py:108
  602.1 0.1 select_reduce_fusion
  602.2 0.2 compare_reduce_fusion
  602.4 0.2 select_bitcast_fusion
  602.6 157.2 %custom-call.8 = f32[8,2,1,128,128]{3,4,2,1,0:T(8,128)S(1)} custom-call(f32[8,2,1,128,128]{4,3,2,1,0:T(8,128)S(1)} %select_bitcast_fusion), custom_call_target="InvertDiagBlocksLowerTriangular" | custom-call | tf_op jit(solution)/shard_map/triangular_solve | solution.py:47
  759.8 1.8 fusion.38
  761.7 1.8 fusion.56
  763.5 0.0 all-to-all-done.1
  763.5 0.0 copy-start.1
  763.5 9.7 %fusion.4 = f32[8,2,128,224]{2,0,3,1:T(8,128)S(1)} fusion(f32[1,2,128,32,224]{2,4,1,0,3:T(8,128)} %all-to-all-done.1, s32[32]{0:T(128)S(1)} %copy-done.4), kind=kOutput, calls=%fused_computation.5 | convolution fusion | flops 176161024 | bytes 9175168 | tf_op jit(solution)/shard_map/em,ebnd->mbnd/dot_general | solution.py:114
  773.3 2.0 fusion.29
  775.3 1.1 copy.127
  776.4 0.0 copy-done.1
  (6 shorter events, 0.1 us)
Async XLA Ops:
  6.5 2.0 copy-start
  6.5 192.3 %all-gather.3.cloned.1.call-start = ((), (), s32[]{:S(2)}) async-start(), calls=%async_computation.3 | async-start | bytes 16515072 | tf_op jit(solution)/shard_map/all_gather | solution.py:73
  45.0 1.9 copy-start.3
  198.9 10.4 %copy-start.5 = (bf16[256,4,7168]{2,0,1:T(8,128)(2,1)S(1)}, bf16[256,4,7168]{2,0,1:T(8,128)(2,1)}, u32[]{:S(2)}) copy-start(bf16[256,4,7168]{2,0,1:T(8,128)(2,1)} %all-gather.3.cloned.1.call-done) | copy-start | bytes 44040196
  233.9 7.9 %copy-start.4 = (s32[32]{0:T(128)S(1)}, s32[32]{0:T(128)}, u32[]{:S(2)}) copy-start(s32[32]{0:T(128)} %param.12) | copy-start | bytes 388
  233.9 529.7 %all-to-all-start.1 = ((f32[1,2,128,32,224]{2,4,1,0,3:T(8,128)}), f32[1,2,128,32,224]{2,4,1,0,3:T(8,128)}, u32[]{:S(2)}, u32[]{:S(2)}) async-start(f32[1,2,128,32,224]{2,4,1,0,3:T(8,128)} %copy.83), calls=%async_computation.1 | async-start | bytes 14680064 | tf_op jit(solution)/shard_map/all_to_all | solution.py:110
  241.8 170.5 %all-reduce.2.cloned.1.call-start = ((), (), s32[]{:S(2)}) async-start(), calls=%async_computation.2 | async-start | bytes 2097152 | tf_op jit(solution)/shard_map/psum | solution.py:107
  412.2 1.8 copy-start.2
  763.5 12.9 %copy-start.1 = (bf16[8,7168]{1,0:T(8,128)(2,1)S(1)}, bf16[8,7168]{1,0:T(8,128)(2,1)}, u32[]{:S(2)}) copy-start(bf16[8,7168]{1,0:T(8,128)(2,1)} %param.7) | copy-start | bytes 344068
Sparse Core Ops, SparseCore 0:
  46.9 151.8 all-gather.2
  245.8 166.4 all-reduce.1
where the time goes:
time: 784 us; the launch traced here: 783 us
  other arithmetic  350 us (45%)
  waiting for transfers between devices  313 us (40%)
  matrix products  51.5 us (7%)
  blocking collectives  34.1 us (4%)
  between operations  13.7 us (2%)
  local copies, waits for them, and re-layouts  12.4 us (2%)
  starting transfers between devices  7.92 us (1%)
    another operation x4, other arithmetic, per_device(): inverse = make_inverse(jnp.linalg.cholesky(build_system(group_gram)))  188 us
    psum x1, waiting for transfers between devices, per_device(): group_gram = lax.psum(placed, 'expert')  168 us
    another operation x3, other arithmetic, make_inverse(): lax.linalg.triangular_solve(factor, unit_matrix, left_side=True, lower=True)  157 us
    all_gather x1, waiting for transfers between devices, per_device(): lax.all_gather(arrived.reshape(1, expert_count, local_experts, capacity,...  146 us
    all_to_all x1, blocking collectives, per_device(): lax.all_to_all(own_slots, 'expert', split_axis=0, concat_axis=0, tiled=True)  34.1 us
  transfers between devices with their start and end apart: 3, of which 2 were waited for; matrix products, arithmetic and copies ran while one was open for 46% of the time, Pallas kernels for 0%

commit v1 on v0

--- a/solution.py
+++ b/solution.py
@@ -70,11 +70,17 @@
     own_slots = slot_maker(routes, tokens).reshape(expert_count, local_experts * capacity, width)
     arrived = lax.all_to_all(own_slots, "expert", split_axis=0, concat_axis=0, tiled=True)
     hidden = activate(
-        lax.all_gather(
-            arrived.reshape(1, expert_count, local_experts, capacity, width),
-            "group",
+        jnp.concatenate(
+            lax.all_to_all(
+                jnp.stack(
+                    [arrived.reshape(1, expert_count, local_experts, capacity, width)]
+                    * lax.axis_size("group")
+                ),
+                "group",
+                0,
+                0,
+            ),
             axis=0,
-            tiled=True,
         ),
         gate_weight,
         up_weight,

time: 784 us -> 962 us (1.23)
  waiting for transfers between devices: 313 us -> 482 us
    all_to_all x0 -> x1, waiting for transfers between devices: none -> 316 us  [per_device(): lax.all_to_all(jnp.stack([arrived.reshape(1, expert_count, local_experts,...]
    all_gather x1 -> x0, waiting for transfers between devices: 146 us -> none  [per_device(): lax.all_gather(arrived.reshape(1, expert_count, local_experts, capacity,...]
  transfers between devices with their start and end apart: 3 -> 3, of which waited for: 2 -> 2; matrix products, arithmetic and copies ran while one was open for 46% -> 37% of each run, Pallas kernels for 0% -> 0%
where the time goes in v1:
time: 962 us; the launch traced here: 961 us
  waiting for transfers between devices  482 us (50%)
  other arithmetic  350 us (36%)
  matrix products  52.8 us (5%)
  blocking collectives  34.1 us (4%)
  local copies, waits for them, and re-layouts  14.7 us (2%)
  starting transfers between devices  13.7 us (1%)
  between operations  13.7 us (1%)
    all_to_all x1, waiting for transfers between devices, per_device(): lax.all_to_all(jnp.stack([arrived.reshape(1, expert_count, local_experts,...  316 us
    another operation x4, other arithmetic, per_device(): inverse = make_inverse(jnp.linalg.cholesky(build_system(group_gram)))  188 us
    psum x1, waiting for transfers between devices, per_device(): group_gram = lax.psum(placed, 'expert')  166 us
    another operation x3, other arithmetic, make_inverse(): lax.linalg.triangular_solve(factor, unit_matrix, left_side=True, lower=True)  157 us
    all_to_all x1, blocking collectives, per_device(): lax.all_to_all(own_slots, 'expert', split_axis=0, concat_axis=0, tiled=True)  34.1 us
  transfers between devices with their start and end apart: 3, of which 2 were waited for; matrix products, arithmetic and copies ran while one was open for 37% of the time, Pallas kernels for 0%

profile of v1, /device:TPU:1, one launch (start us, length us, event | category | flops | bytes accessed | tf_op | source)
XLA Modules:
  0.0 961.2 jit_solution(10924694266690464195)
XLA Ops:
  6.5 0.0 copy-start
  6.5 0.8 eq.91
  7.3 0.1 fusion.51
  7.4 0.1 reduce_window_sum.11
  7.5 0.2 select_reduce_fusion.1
  7.7 0.1 reduce_sum.21
  7.8 0.7 multiply_add_fusion
  8.5 0.1 convert_reduce_fusion
  8.6 0.0 copy-done
  8.6 0.7 convolution_convert_fusion
  9.3 1.7 reshape.140
  10.9 34.1 %all_to_all.25 = bf16[32,4,7168]{2,1,0:T(4,128)(2,1)S(1)} all-to-all(bf16[32,4,7168]{2,1,0:T(4,128)(2,1)} %reshape.140), channel_id=1, replica_groups=mesh['expert'=32,'group'=8] {'expert'}, dimensions={0} | all-to-all | bytes 3670016 | tf_op jit(solution)/shard_map/all_to_all | solution.py:71
  45.0 0.5 copy.61
  45.5 5.5 stack.3
  51.0 0.0 copy-start.3
  51.0 8.3 all-to-all-start.1
  59.3 0.0 copy-done.3
  59.4 0.1 broadcast_subtract_fusion
  59.4 6.2 fusion.44
  65.6 316.2 %all-to-all-done.1 = bf16[8,1,32,1,4,7168]{5,2,4,3,1,0:T(8,128)(2,1)} async-done(((bf16[8,1,32,1,4,7168]{5,2,4,3,1,0:T(8,128)(2,1)}), bf16[8,1,32,1,4,7168]{5,2,4,3,1,0:T(8,128)(2,1)}, u32[]{:S(2)}, u32[]{:S(2)}) %all-to-all-start.1) | async-done | bytes 14680096 | tf_op jit(solution)/shard_map/all_to_all | solution.py:74
  381.8 0.0 copy-start.5
  381.8 8.5 fusion.14
  390.3 0.0 copy-done.5
  390.3 7.5 fusion.32
  397.8 0.1 reshape.144
  398.0 0.4 fusion.37
  398.3 0.3 convolution_bitcast_fusion
  398.7 13.8 %fusion.57 = f32[2,128,7168]{1,2,0:T(8,128)S(1)} fusion(f32[2,128,128]{2,1,0:T(8,128)S(1)} %convolution_bitcast_fusion, f32[2,128,7168]{2,1,0:T(8,128)} %fusion.44), kind=kOutput, calls=%fused_computation.58 | convolution fusion | flops 2818572288 | bytes 14811136 | tf_op jit(solution)/shard_map/jbni,jbid->jbnd/dot_general | solution.py:106
  412.5 3.7 copy.76
  416.2 0.0 copy-start.4
  416.2 5.3 all-to-all-start.2
  421.5 0.0 all-reduce.2.cloned.1.call-start
  421.6 0.0 copy-done.4
  421.6 0.6 dynamic_slice.3
  422.2 0.6 compare_convert_fusion
  422.8 0.1 copy.66
  422.9 1.2 broadcast_multiply_fusion
  424.1 0.0 all-reduce.2.cloned.1.call-update
  424.1 0.1 copy.67
  424.2 0.1 copy.68
  424.4 166.0 %all-reduce.2.cloned.1.call-done = f32[8,2,128,128]{2,3,1,0:T(8,128)} async-done(((f32[8,2,128,128]{2,3,1,0:T(8,128)}), f32[8,2,128,128]{2,3,1,0:T(8,128)}) %all-reduce.2.cloned.1.call-update) | async-done | bytes 1048592 | tf_op jit(solution)/shard_map/psum | solution.py:113
  590.4 0.0 copy-start.2
  590.4 1.5 add_add_fusion
  591.9 0.3 copy.69
  592.2 0.0 copy-done.2
  592.2 0.2 fusion.40
  592.5 187.6 %custom-call.7 = f32[8,2,128,128]{3,2,1,0:T(8,128)S(1)} custom-call(f32[8,2,128,128]{3,2,1,0:T(8,128)S(1)} %fusion.40), custom_call_target="Cholesky" | custom-call | tf_op jit(solution)/shard_map/jit(cholesky)/cholesky | solution.py:114
  780.0 0.1 select_reduce_fusion
  780.1 0.2 compare_reduce_fusion
  780.3 0.2 select_bitcast_fusion
  780.6 157.2 %custom-call.8 = f32[8,2,1,128,128]{3,4,2,1,0:T(8,128)S(1)} custom-call(f32[8,2,1,128,128]{4,3,2,1,0:T(8,128)S(1)} %select_bitcast_fusion), custom_call_target="InvertDiagBlocksLowerTriangular" | custom-call | tf_op jit(solution)/shard_map/triangular_solve | solution.py:47
  937.8 1.8 fusion.38
  939.6 1.8 fusion.56
  941.4 0.0 all-to-all-done.2
  941.5 0.0 copy-start.1
  941.5 9.7 %fusion.4 = f32[8,2,128,224]{2,0,3,1:T(8,128)S(1)} fusion(f32[1,2,128,32,224]{2,4,1,0,3:T(8,128)} %all-to-all-done.2, s32[32]{0:T(128)S(1)} %copy-done.4), kind=kOutput, calls=%fused_computation.5 | convolution fusion | flops 176161024 | bytes 9175168 | tf_op jit(solution)/shard_map/em,ebnd->mbnd/dot_general | solution.py:120
  951.2 2.0 fusion.29
  953.2 1.1 copy.108
  954.3 0.0 copy-done.1
  (6 shorter events, 0.1 us)
Async XLA Ops:
  6.5 2.0 copy-start
  51.0 8.3 copy-start.3
  51.0 330.7 %all-to-all-start.1 = ((bf16[8,1,32,1,4,7168]{5,2,4,3,1,0:T(8,128)(2,1)}), bf16[8,1,32,1,4,7168]{5,2,4,3,1,0:T(8,128)(2,1)}, u32[]{:S(2)}, u32[]{:S(2)}) async-start(bf16[8,1,32,1,4,7168]{5,2,4,3,1,0:T(8,128)(2,1)} %stack.3), calls=%async_computation.1 | async-start | bytes 29360128 | tf_op jit(solution)/shard_map/all_to_all | solution.py:74
  381.8 8.5 copy-start.5
  416.2 5.4 copy-start.4
  416.2 525.2 %all-to-all-start.2 = ((f32[1,2,128,32,224]{2,4,1,0,3:T(8,128)}), f32[1,2,128,32,224]{2,4,1,0,3:T(8,128)}, u32[]{:S(2)}, u32[]{:S(2)}) async-start(f32[1,2,128,32,224]{2,4,1,0,3:T(8,128)} %copy.76), calls=%async_computation.2 | async-start | bytes 14680064 | tf_op jit(solution)/shard_map/all_to_all | solution.py:116
  421.5 168.9 %all-reduce.2.cloned.1.call-start = ((), (), s32[]{:S(2)}) async-start(), calls=%async_computation.3 | async-start | bytes 2097152 | tf_op jit(solution)/shard_map/psum | solution.py:113
  590.4 1.8 copy-start.2
  941.5 12.9 %copy-start.1 = (bf16[8,7168]{1,0:T(8,128)(2,1)S(1)}, bf16[8,7168]{1,0:T(8,128)(2,1)}, u32[]{:S(2)}) copy-start(bf16[8,7168]{1,0:T(8,128)(2,1)} %param.7) | copy-start | bytes 344068
Sparse Core Ops, SparseCore 0:
  425.6 164.7 all-reduce.1
